TPU v7x, 256 devices: a whole 4x4x8 slice. The times are simulated.
256 devices in a mesh: gx: 8 (over z), gy: 16 (over y, x), sa: 2 (over core).
Axes of the slice: x: 4, y: 4, z: 8, core: 2. Of those that a mesh axis runs over, the one named last changes fastest.
Arguments:
- field: float32 [33, 32, 672, 256], P(None, 'gx', 'gy', 'sa'), as said below
- start: float32 [33, 16], replicated, may hold values from -1 to 1
Outputs:
- basis: float32 [33, 16], replicated
- gram_two: float32 [672, 672], P('gy', ('gx', 'sa'))
Inputs may be any that keep to these rules, and one draw needn't show every extreme that they name: `field`: every entry is finite; species differ in scale.
All inputs are finite; a program needn't handle non-finite values.
Results may differ from a plain program's by a relative error of at most 0.0003.
Values sent between devices are 32-bit elements; how exact they have to be, the bound alone decides.
A program may use at most 128 MiB of HBM per device.

v0:
```python
import jax
import jax.numpy as jnp
from jax import lax
from jax.sharding import PartitionSpec as P

ITERS = 4


HIGH = lax.Precision.HIGHEST


def orth(block):
    inner = jnp.dot(block.T, block, precision=HIGH, preferred_element_type=jnp.float32)
    lower = jnp.linalg.cholesky(inner)
    return jax.scipy.linalg.solve_triangular(lower, block.T, lower=True).T


def leading(gram, start, rounds):
    basis = orth(orth(start))
    for step in range(rounds):
        basis = orth(orth(jnp.dot(gram, basis, precision=HIGH, preferred_element_type=jnp.float32)))
    return basis


def project(basis, data):
    return jnp.einsum("sr,sxyz->rxyz", basis, data, precision=HIGH)


def line_gram(left, right):
    return jnp.einsum("rxiz,rxjz->ij", left, right, precision=HIGH)


def on_device(field, start):
    species, cells_x, cells_y, cells_z = field.shape
    ranks = start.shape[1]
    total_x = cells_x * lax.axis_size("gx")
    total_y = cells_y * lax.axis_size("gy")
    total_z = cells_z * lax.axis_size("sa")
    flat = field.reshape(species, -1)
    partial_gram = jnp.dot(flat, flat.T, precision=HIGH, preferred_element_type=jnp.float32)
    species_gram = lax.psum(partial_gram, ("gx", "gy", "sa")) / (total_x * total_y * total_z)
    basis = leading(species_gram, start, ITERS)
    core = project(basis, field)
    part_block = line_gram(core, lax.all_gather(core, "gy", axis=2, tiled=True))
    block = lax.psum_scatter(part_block, ("gx", "sa"), scatter_dimension=1, tiled=True) / (
        ranks * total_x * total_z
    )
    return (basis, block)


def solution(mesh):
    in_specs = (P(None, "gx", "gy", "sa"), P())
    out_specs = (P(), P("gy", ("gx", "sa")))
    return jax.shard_map(
        on_device, mesh=mesh, in_specs=in_specs, out_specs=out_specs, check_vma=False
    )
```

profile of v0, /device:TPU:8, one launch (start us, length us, event | category | flops | bytes accessed | tf_op | source)
XLA Modules:
  0.0 421.3 jit_solution(17980562996375337005)
XLA Ops:
  8.1 1.5 cholesky.164
  10.9 1.2 custom-call.14
  12.5 1.5 cholesky.175
  15.3 1.2 custom-call.15
  16.8 6.2 %fusion.12 = f32[33,33]{1,0:T(8,128)S(1)} fusion(f32[33,4,42,128]{3,1,2,0:T(4,128)} %param.5), kind=kOutput, calls=%fused_computation.8 | convolution fusion | flops 281014272 | bytes 2842884 | tf_op jit(solution)/shard_map/dot_general | solution.py:40
  22.9 78.7 %psum.7 = f32[33,33]{1,0:T(8,128)S(1)} all-reduce(f32[33,33]{1,0:T(8,128)S(1)} %fusion.12), channel_id=1, replica_groups=mesh['gx'=8,'gy'=16,'sa'=2] {'gx','gy','sa'}, use_global_device_ids=true, to_apply=%region_0.0 | all-reduce | flops 1089 | bytes 8712 | tf_op jit(solution)/shard_map/psum | solution.py:41
  102.0 1.5 cholesky.186
  104.8 1.2 custom-call.16
  106.5 1.5 cholesky.197
  109.3 1.2 custom-call.17
  111.1 1.5 cholesky.208
  113.9 1.2 custom-call.18
  115.5 1.5 cholesky.219
  118.3 1.2 custom-call.19
  120.1 1.5 cholesky.230
  123.0 1.2 custom-call.20
  124.6 1.5 cholesky.241
  129.2 1.5 cholesky.252
  133.7 1.5 cholesky.263
  137.9 3.4 fusion.2
  141.6 140.0 %all-gather.2.cloned.1.call-done = f32[16,4,672,128]{3,0,2,1:T(8,128)} async-done(((f32[16,4,42,128]{3,0,2,1:T(8,128)}), f32[16,4,672,128]{3,0,2,1:T(8,128)}) %all-gather.2.cloned.1.call-update) | async-done | bytes 22020112 | tf_op jit(solution)/shard_map/all_gather | solution.py:44
  281.6 29.2 %fusion.7 = f32[42,672]{1,0:T(8,128)} fusion(f32[16,4,672,128]{3,0,2,1:T(8,128)} %all-gather.2.cloned.1.call-done, f32[16,4,42,128]{3,0,2,1:T(8,128)} %fusion.2), kind=kOutput, calls=%fused_computation.7 | convolution fusion | flops 2774532096 | bytes 23509248 | tf_op jit(solution)/shard_map/rxiz,rxjz->ij/dot_general | solution.py:30
  312.1 100.9 %all-reduce.3.cloned.1.call-done = f32[42,672]{1,0:T(8,128)} async-done(((f32[42,672]{1,0:T(8,128)}), f32[42,672]{1,0:T(8,128)}) %all-reduce.3.cloned.1.call-update) | async-done | bytes 112912
  413.0 1.5 dynamic-slice_multiply_fusion
  (90 shorter events, 23.3 us)
Async XLA Ops:
  7.2 0.7 copy-start
  7.2 130.7 %copy-start.1 = (f32[33,4,42,128]{3,1,2,0:T(4,128)S(1)}, f32[33,4,42,128]{3,1,2,0:T(4,128)}, u32[]{:S(2)}) copy-start(f32[33,4,42,128]{3,1,2,0:T(4,128)} %param.5) | copy-start | bytes 8515588
  7.2 274.4 %all-gather.2.cloned.1.call-start = ((), (), s32[]{:S(2)}) async-start(), calls=%async_computation | async-start | bytes 23396352 | tf_op jit(solution)/shard_map/all_gather | solution.py:44
  137.9 3.4 copy-start.2
  141.4 169.5 %copy-start.3 = (u32[256]{0:T(256)S(1)}, u32[256]{0:T(256)}, u32[]{:S(2)}) copy-start(u32[256]{0:T(256)} %constant.40) | copy-start | bytes 3076
  141.4 271.6 %all-reduce.3.cloned.1.call-start = ((), (), s32[]{:S(2)}) async-start(), calls=%async_computation.1 | async-start | bytes 294912
Sparse Core Ops, SparseCore 0:
  141.5 140.1 all-gather.1
  310.9 101.9 all-reduce.2
where the time goes:
time: 423 us; the launch traced here: 421 us
  waiting for transfers between devices  241 us (57%)
  blocking collectives  78.7 us (19%)
  matrix products  42.7 us (10%)
  other arithmetic  41.8 us (10%)
  between operations  14.9 us (4%)
    all_gather x1, waiting for transfers between devices, on_device(): part_block = line_gram(core, lax.all_gather(core, 'gy', axis=2, tiled=True))  140 us
    unnamed x3, waiting for transfers between devices  101 us
    psum x1, blocking collectives, on_device(): lax.psum(partial_gram, ('gx', 'gy', 'sa')) / (total_x * total_y * total_z)  78.7 us
    dot_general x1, matrix products, line_gram(): return jnp.einsum('rxiz,rxjz->ij', left, right, precision=HIGH)  29.2 us
    another operation x30, other arithmetic, orth(): lower = jnp.linalg.cholesky(inner)  21.5 us
    another operation x20, other arithmetic, orth(): return jax.scipy.linalg.solve_triangular(lower, block.T, lower=True).T  18.8 us
  transfers between devices with their start and end apart: 2, of which 2 were waited for; matrix products, arithmetic and copies ran while one was open for 0% of the time, Pallas kernels for 0%

commit v1 on v0

v1 whole, which is shorter than its diff:
```python
import functools
import math

import jax
import jax.numpy as jnp
from jax import lax
from jax.experimental import pallas as pl
from jax.experimental.pallas import tpu as pltpu
from jax.sharding import PartitionSpec as P

ITERS = 4
F32 = jnp.float32
BF16 = jnp.bfloat16
HIGH = lax.Precision.HIGHEST
LANES = 128
SP = 48
YP = 48
NT = (((1,), (1,)), ((), ()))


def split(value):
    high = value.astype(BF16)
    return high, (value - high.astype(F32)).astype(BF16)


def orth(w, ranks):
    products = (w[:, None, :] * w[None, :, :]).reshape(ranks * ranks, LANES)
    first, rest = split(products)
    second, third = split(products - first.astype(F32))
    ones = jnp.ones((LANES, LANES), BF16)
    inner = (
        jnp.dot(first, ones, preferred_element_type=F32)
        + jnp.dot(second, ones, preferred_element_type=F32)
        + jnp.dot(third, ones, preferred_element_type=F32)
    )
    lines = [inner[i * ranks : (i + 1) * ranks] for i in range(ranks)]
    row = lax.broadcasted_iota(jnp.int32, (ranks, LANES), 0)
    pivots = jnp.ones((ranks, LANES), F32)
    for j in range(ranks):
        line = lines[j]
        pivots = jnp.where(row == j, line, pivots)
        factor = line * (1.0 / line[j : j + 1])
        if j + 1 < ranks:
            below = jnp.where(row > j, factor, 0.0)
            w = w - below * w[j : j + 1]
            for i in range(j + 1, ranks):
                lines[i] = lines[i] - factor[i : i + 1] * line
    return w * lax.rsqrt(pivots)


def kernel(cfg, field, start, basis_out, block_out, fv, hl, ub, zb, b_sa, b_x, b_y, b_z,
           core, mid0, mid1, recv, ah, al, gs, go, gr, r1a, r1b, t0, t1, r2a, r2b, hb, pack, r3,
           load_sem, ssem, rsem):
    nx, ny, nz, ns = cfg["nx"], cfg["ny"], cfg["nz"], 2
    species, cx, cy, cz = field.shape
    ranks = start.shape[1]
    gx, gy, sa = lax.axis_index("gx"), lax.axis_index("gy"), lax.axis_index("sa")
    mx, my = lax.rem(gy, nx), gy // nx

    def to_sa(d):
        return {"sa": 1 - sa}

    def to_x(d):
        return {"gy": my * nx + lax.rem(mx + d, nx)}

    def to_y(d):
        return {"gy": lax.rem(my + d, ny) * nx + mx}

    def to_z(d):
        return {"gx": lax.rem(gx + d, nz)}

    used = [0]

    def send(src, dst, target):
        k = used[0]
        used[0] += 1
        copy = pltpu.make_async_remote_copy(
            src_ref=src, dst_ref=dst, send_sem=ssem.at[k], recv_sem=rsem.at[k],
            device_id=target, device_id_type=pl.DeviceIdType.MESH,
        )
        copy.start()
        return copy

    load = pltpu.make_async_copy(field, fv.at[0:species, :, 0:cy, :], load_sem)
    load.start()
    barrier = pltpu.get_barrier_semaphore()
    peers = [to_sa(1)] + [to_x(d) for d in range(1, nx)] + [to_y(d) for d in range(1, ny)]
    peers += [to_z(d) for d in range(1, nz)]
    for peer in peers:
        pl.semaphore_signal(barrier, inc=1, device_id=peer, device_id_type=pl.DeviceIdType.MESH)
    fv[species:SP] = jnp.zeros((SP - species, cx, YP, cz), F32)
    ub[...] = jnp.zeros(ub.shape, F32)
    zb[...] = jnp.zeros(zb.shape, F32)
    zb[0:species, 0:ranks] = start[...]
    load.wait()

    flat = fv.reshape(SP * cx * YP, cz)
    step = cfg["step"]
    wide = step * cz
    total = jnp.zeros((2 * SP, SP), F32)
    for x in range(cx):
        for g in range(cy // step):
            cols = [flat[pl.ds(x * YP + g * step + k, SP, stride=cx * YP), :] for k in range(step)]
            high, low = split(jnp.concatenate(cols, axis=1))
            both = jnp.concatenate([high, low], axis=0)
            at = (x * (cy // step) + g) * wide
            hl[:, at : at + wide] = both
            total = total + lax.dot_general(both, high, NT, preferred_element_type=F32)
    ub[0:SP, 0:SP] = total[0:SP] * 0.5 + total[SP:]
    lane = lax.broadcasted_iota(jnp.int32, (SP, LANES), 1)
    half = ub[...]
    packed = half[0:16] + pltpu.roll(half[16:32], 42, 1) + pltpu.roll(half[32:48], 84, 1)

    pl.semaphore_wait(barrier, len(peers))

    def start_sum(value, buf, n, me, target):
        buf[me] = value
        return [send(buf.at[me], buf.at[me], target(d)) for d in range(1, n)]

    def end_sum(copies, buf, n):
        for copy in copies:
            copy.wait()
        out = buf[0]
        for k in range(1, n):
            out = out + buf[k]
        return out

    packed = end_sum(start_sum(packed, b_sa, ns, sa, to_sa), b_sa, ns)
    packed = end_sum(start_sum(packed, b_x, nx, mx, to_x), b_x, nx)
    packed = end_sum(start_sum(packed, b_y, ny, my, to_y), b_y, ny)
    copies = start_sum(packed, b_z, nz, gx, to_z)
    w = zb[...].T[0:ranks]
    w = orth(orth(w, ranks), ranks)
    packed = end_sum(copies, b_z, nz)

    scale = 1.0 / cfg["cells"]
    packed = packed * scale
    ub[0:16] = packed
    ub[16:32] = pltpu.roll(packed, LANES - 42, 1)
    ub[32:48] = pltpu.roll(packed, LANES - 84, 1)
    srow = lax.broadcasted_iota(jnp.int32, (SP, LANES), 0)
    half = jnp.where((lane < species) & (srow < species), ub[...], 0.0)
    zb[...] = jnp.zeros(zb.shape, F32)
    zb[0:SP] = half
    half = zb[...]
    gram = half + half.T

    def round_(i, w):
        w = jnp.dot(w, gram, precision=HIGH, preferred_element_type=F32)
        return orth(orth(w, ranks), ranks)

    w = lax.fori_loop(0, ITERS, round_, w)

    whigh = w.astype(BF16).astype(F32)
    lhs = jnp.concatenate([whigh + pltpu.roll(whigh, SP, 1), w - whigh], axis=0).astype(BF16)
    lhs = lhs[:, 0 : 2 * SP]
    cflat = core.reshape(ranks * cx * YP, cz)

    def project(x):
        for g in range(cy // step):
            at = (x * (cy // step) + g) * wide
            out = jnp.dot(lhs, hl[:, at : at + wide], preferred_element_type=F32)
            out = out[0:ranks] + out[ranks:]
            for k in range(step):
                cflat[pl.ds(x * YP + g * step + k, ranks, stride=cx * YP), :] = (
                    out[:, k * cz : (k + 1) * cz]
                )

    hx = cx // 2
    for x in range(hx):
        project(x)
    first0 = []
    for d in range(1, nx):
        there = lax.rem(mx + d, nx)
        first0.append(send(core.at[:, there, 0:hx, 0:cy, :], mid0.at[:, :, mx, 0:cy, :], to_x(d)))
    for x in range(hx, cx):
        project(x)
    first1 = []
    for d in range(1, ny):
        there = lax.rem(my + d, ny)
        first1.append(send(core.at[there, :, hx:cx, 0:cy, :], mid1.at[:, :, my, 0:cy, :], to_y(d)))
    mid0[:, :, mx] = core[:, mx, 0:hx]
    mid1[:, :, my] = core[my, :, hx:cx]
    zb[0:ranks] = w
    basis_out[...] = zb[...].T[0:species, 0:ranks]
    for copy in first0:
        copy.wait()
    second = []
    for d in range(1, ny):
        there = lax.rem(my + d, ny)
        second.append(send(mid0.at[there, :, :, 0:cy, :], recv.at[0:hx, my, :, 0:cy, :], to_y(d)))
    recv[0:hx, my] = mid0[my]
    for copy in first1:
        copy.wait()
    for d in range(1, nx):
        there = lax.rem(mx + d, nx)
        second.append(send(mid1.at[there, :, :, 0:cy, :], recv.at[hx:cx, :, mx, 0:cy, :], to_x(d)))
    recv[hx:cx, :, mx] = mid1[mx]
    for copy in second:
        copy.wait()

    rows = ny * nx * YP
    for x in range(cx):
        high, low = split(recv[x].reshape(rows, cz))
        ah[:, :, :, x * cz : (x + 1) * cz] = high.reshape(nz, ns, YP, cz)
        al[:, :, :, x * cz : (x + 1) * cz] = low.reshape(nz, ns, YP, cz)
    depth = cx * cz
    columns = nz * YP
    lrows = ah.reshape(ny, nx * YP, depth), al.reshape(ny, nx * YP, depth)

    def gram_rows(y, side):
        lh, ll = lrows[0][y], lrows[1][y]
        rh, rl = ah[:, side].reshape(columns, depth), al[:, side].reshape(columns, depth)
        out = (
            lax.dot_general(lh, rh, NT, preferred_element_type=F32)
            + lax.dot_general(lh, rl, NT, preferred_element_type=F32)
            + lax.dot_general(ll, rh, NT, preferred_element_type=F32)
        )
        return out.reshape(nx, YP, columns)

    swaps = []
    for y in range(ny):
        gs[y] = gram_rows(y, 1 - sa)
        swaps.append(send(gs.at[y], gr.at[y], to_sa(1)))
    for y in range(ny):
        mine = gram_rows(y, sa)
        swaps[y].wait()
        go[y] = mine + gr[y]

    hy = YP // 2
    first0 = []
    for d in range(1, nx):
        there = lax.rem(mx + d, nx)
        first0.append(send(go.at[:, there, 0:hy, :], r1a.at[d - 1], to_x(d)))
    first1 = []
    for d in range(1, ny):
        there = lax.rem(my + d, ny)
        first1.append(send(go.at[there, :, hy:YP, :], r1b.at[d - 1], to_y(d)))
    for copy in first0:
        copy.wait()
    out = go[:, mx, 0:hy, :]
    for d in range(1, nx):
        out = out + r1a[d - 1]
    t0[...] = out
    second0 = []
    for d in range(1, ny):
        second0.append(send(t0.at[lax.rem(my + d, ny)], r2a.at[d - 1], to_y(d)))
    for copy in first1:
        copy.wait()
    out = go[my, :, hy:YP, :]
    for d in range(1, ny):
        out = out + r1b[d - 1]
    t1[...] = out
    second1 = []
    for d in range(1, nx):
        second1.append(send(t1.at[lax.rem(mx + d, nx)], r2b.at[d - 1], to_x(d)))
    for copy in second0:
        copy.wait()
    out = t0[my]
    for d in range(1, ny):
        out = out + r2a[d - 1]
    hb[0:hy, 0 : nz * YP] = out
    for copy in second1:
        copy.wait()
    out = t1[mx]
    for d in range(1, nx):
        out = out + r2b[d - 1]
    hb[hy:YP, 0 : nz * YP] = out

    fold = lax.broadcasted_iota(jnp.int32, (hy, LANES), 1) < LANES // 2
    for g in range(nz):
        tile = (g * YP) // LANES
        at = g * YP - tile * LANES
        parts = []
        for part in (hb[0:hy], hb[hy:YP]):
            piece = part[:, tile * LANES : (tile + 1) * LANES]
            if at:
                piece = pltpu.roll(piece, LANES - at, 1)
            if at + YP > LANES:
                other = part[:, (tile + 1) * LANES : (tile + 2) * LANES]
                where = lax.broadcasted_iota(jnp.int32, (hy, LANES), 1) < LANES - at
                piece = jnp.where(where, piece, pltpu.roll(other, LANES - at, 1))
            parts.append(piece)
        pack[g] = jnp.where(fold, parts[0], pltpu.roll(parts[1], LANES // 2, 1))
    last = []
    for d in range(1, nz):
        last.append(send(pack.at[lax.rem(gx + d, nz)], r3.at[d - 1], to_z(d)))
    out = pack[gx]
    for copy in last:
        copy.wait()
    for d in range(1, nz):
        out = out + r3[d - 1]
    out = out * (1.0 / cfg["terms"])
    block_out[0:hy, :] = out[:, 0:cy]
    block_out[hy:cy, :] = pltpu.roll(out, LANES // 2, 1)[0 : cy - hy, 0:cy]


def on_device(cfg, field, start):
    species, cx, cy, cz = field.shape
    ranks = start.shape[1]
    nx, ny, nz = cfg["nx"], cfg["ny"], cfg["nz"]
    cols = nz * YP
    colsp = -(-cols // LANES) * LANES
    hy = YP // 2
    hx = cx // 2
    cells = cx * cy * cz
    copies = 1 + (nx - 1) + (ny - 1) + (nz - 1) + 2 * (nx + ny - 2) + ny + 2 * (nx + ny - 2) + nz - 1
    vmem = pltpu.VMEM
    scratch = [
        vmem((SP, cx, YP, cz), F32), vmem((2 * SP, cells), BF16), vmem((SP, LANES), F32),
        vmem((LANES, LANES), F32), vmem((2, 16, LANES), F32), vmem((nx, 16, LANES), F32),
        vmem((ny, 16, LANES), F32), vmem((nz, 16, LANES), F32),
        vmem((ny, nx, cx, YP, cz), F32), vmem((ny, hx, nx, YP, cz), F32),
        vmem((nx, hx, ny, YP, cz), F32), vmem((cx, ny, nx, YP, cz), F32),
        vmem((nz, 2, YP, cx * cz), BF16), vmem((nz, 2, YP, cx * cz), BF16),
        vmem((ny, nx, YP, cols), F32), vmem((ny, nx, YP, cols), F32), vmem((ny, nx, YP, cols), F32),
        vmem((nx - 1, ny, hy, cols), F32), vmem((ny - 1, nx, hy, cols), F32),
        vmem((ny, hy, cols), F32), vmem((nx, hy, cols), F32),
        vmem((ny - 1, hy, cols), F32), vmem((nx - 1, hy, cols), F32),
        vmem((YP, colsp), F32), vmem((nz, hy, LANES), F32), vmem((nz - 1, hy, LANES), F32),
        pltpu.SemaphoreType.DMA, pltpu.SemaphoreType.DMA((copies,)), pltpu.SemaphoreType.DMA((copies,)),
    ]
    return pl.pallas_call(
        functools.partial(kernel, cfg),
        out_shape=(
            jax.ShapeDtypeStruct((species, ranks), F32),
            jax.ShapeDtypeStruct((cy, cy), F32),
        ),
        in_specs=[pl.BlockSpec(memory_space=pl.ANY), pl.BlockSpec(memory_space=vmem)],
        out_specs=(pl.BlockSpec(memory_space=vmem), pl.BlockSpec(memory_space=vmem)),
        scratch_shapes=scratch,
        compiler_params=pltpu.CompilerParams(
            collective_id=0, has_side_effects=True, vmem_limit_bytes=56 * 1024 * 1024
        ),
        name="tucker_step",
    )(field, start)


def solution(mesh):
    nz, n_plane, ns = mesh.shape["gx"], mesh.shape["gy"], mesh.shape["sa"]
    nx = math.isqrt(n_plane)
    cfg = dict(nx=nx, ny=n_plane // nx, nz=nz)

    def run(field, start):
        species, cx, cy, cz = field.shape
        ranks = start.shape[1]
        total = cx * nz * cz * ns
        full = dict(cfg, step=14 if cy % 14 == 0 else cy, cells=total * cy * n_plane, terms=ranks * total)
        return on_device(full, field, start)

    return jax.shard_map(
        run, mesh=mesh, in_specs=(P(None, "gx", "gy", "sa"), P()),
        out_specs=(P(), P("gy", ("gx", "sa"))), check_vma=False,
    )
```

time: 423 us -> 79.5 us (0.19)
  waiting for transfers between devices: 241 us -> 0 us
  blocking collectives: 78.7 us -> 0 us
  Pallas kernels: 0 us -> 70.6 us
  matrix products: 42.7 us -> 0 us
  other arithmetic: 41.8 us -> 0 us
  between operations: 14.9 us -> 0.64 us
  local copies, waits for them, and re-layouts: 1.98 us -> 7.91 us
    all_gather x1 -> x0, waiting for transfers between devices: 140 us -> none  [on_device(): part_block = line_gram(core, lax.all_gather(core, 'gy', axis=2, tiled=True))]
    unnamed x3 -> x0, waiting for transfers between devices: 101 us -> none
    psum x1 -> x0, blocking collectives: 78.7 us -> none  [on_device(): lax.psum(partial_gram, ('gx', 'gy', 'sa')) / (total_x * total_y * total_z)]
    pallas_call x0 -> x1, Pallas kernels: none -> 70.6 us  [on_device(): pl.pallas_call(functools.partial(kernel, cfg), out_shape=(jax.ShapeDtypeS...]
    dot_general x17 -> x0, matrix products: 40.7 us -> none  [the longest x1 29.2 us: line_gram(): return jnp.einsum('rxiz,rxjz->ij', left, right, precision=HIGH)]
    another operation x50 -> x0, other arithmetic: 40.2 us -> none  [the longest x30 21.5 us: orth(): lower = jnp.linalg.cholesky(inner)]
    unnamed x9 -> x3, local copies, waits for them, and re-layouts: 1.25 us -> 6.51 us
  transfers between devices with their start and end apart: 2 -> 0, of which waited for: 2 -> 0; matrix products, arithmetic and copies ran while one was open for 0% -> 0% of each run, Pallas kernels for 0% -> 0%
where the time goes in v1:
time: 79.5 us; the launch traced here: 79.1 us
  Pallas kernels  70.6 us (89%)
  local copies, waits for them, and re-layouts  7.91 us (10%)
    pallas_call x1, Pallas kernels, on_device(): pl.pallas_call(functools.partial(kernel, cfg), out_shape=(jax.ShapeDtypeS...  70.6 us
    unnamed x3, local copies, waits for them, and re-layouts  6.51 us

profile of v1, /device:TPU:8, one launch (start us, length us, event | category | flops | bytes accessed | tf_op | source)
XLA Modules:
  0.0 79.1 jit_solution(18113884467531044485)
XLA Ops:
  0.6 1.4 %copy.5.start = f32[33,16]{1,0:T(8,128)} copy(f32[33,16]{0,1:T(8,128)} %param.3) | data formatting | bytes 4224 | tf_op args[1]
  2.0 3.8 %copy.4.field = f32[33,4,42,128]{3,2,1,0:T(8,128)} copy(f32[33,4,42,128]{3,1,2,0:T(4,128)} %param.2) | data formatting | bytes 5677056 | tf_op args[0]
  5.8 70.6 %tucker_step.1 = (f32[33,16]{1,0:T(8,128)}, f32[42,42]{1,0:T(8,128)}) custom-call(f32[33,4,42,128]{3,2,1,0:T(8,128)} %copy.4.field, f32[33,16]{1,0:T(8,128)} %copy.5.start), custom_call_target="tpu_custom_call" | custom-call | tf_op jit(solution)/shard_map/tucker_step/pallas_call | solution.py:323
  76.4 1.4 %copy.6 = f32[33,16]{0,1:T(8,128)} copy(f32[33,16]{1,0:T(8,128)} %get-tuple-element.2) | data formatting | bytes 4224 | tf_op jit(solution)/shard_map/tucker_step/pallas_call | solution.py:323
  77.8 1.3 %copy.8 = f32[42,42]{1,0:T(8,128)} copy(f32[42,42]{1,0:T(8,128)} %get-tuple-element.7) | data formatting | bytes 14112

commit v2 on v1

--- a/solution.py
+++ b/solution.py
@@ -48,12 +48,13 @@
     return w * lax.rsqrt(pivots)
 
 
-def kernel(cfg, field, start, basis_out, block_out, fv, hl, ub, zb, b_sa, b_x, b_y, b_z,
+def kernel(cfg, field, start, both_out, fv, hl, ub, zb, wb, b_sa, b_p, b_z,
            core, mid0, mid1, recv, ah, al, gs, go, gr, r1a, r1b, t0, t1, r2a, r2b, hb, pack, r3,
            load_sem, ssem, rsem):
     nx, ny, nz, ns = cfg["nx"], cfg["ny"], cfg["nz"], 2
-    species, cx, cy, cz = field.shape
-    ranks = start.shape[1]
+    species, cz = field.shape[0], field.shape[2]
+    cx, cy = cfg["cx"], cfg["cy"]
+    ranks = start.shape[0]
     gx, gy, sa = lax.axis_index("gx"), lax.axis_index("gy"), lax.axis_index("sa")
     mx, my = lax.rem(gy, nx), gy // nx
 
@@ -65,6 +66,9 @@
 
     def to_y(d):
         return {"gy": lax.rem(my + d, ny) * nx + mx}
+
+    def to_plane(d):
+        return {"gy": lax.rem(my + d // nx, ny) * nx + lax.rem(mx + d % nx, nx)}
 
     def to_z(d):
         return {"gx": lax.rem(gx + d, nz)}
@@ -81,26 +85,26 @@
         copy.start()
         return copy
 
-    load = pltpu.make_async_copy(field, fv.at[0:species, :, 0:cy, :], load_sem)
+    load = pltpu.make_async_copy(field, fv.at[0:species], load_sem)
     load.start()
     barrier = pltpu.get_barrier_semaphore()
-    peers = [to_sa(1)] + [to_x(d) for d in range(1, nx)] + [to_y(d) for d in range(1, ny)]
+    peers = [to_sa(1)] + [to_plane(d) for d in range(1, nx * ny)]
     peers += [to_z(d) for d in range(1, nz)]
     for peer in peers:
         pl.semaphore_signal(barrier, inc=1, device_id=peer, device_id_type=pl.DeviceIdType.MESH)
-    fv[species:SP] = jnp.zeros((SP - species, cx, YP, cz), F32)
+    fv[species:SP] = jnp.zeros((SP - species, cx * cy, cz), F32)
     ub[...] = jnp.zeros(ub.shape, F32)
-    zb[...] = jnp.zeros(zb.shape, F32)
-    zb[0:species, 0:ranks] = start[...]
+    wb[...] = jnp.zeros(wb.shape, F32)
+    wb[:, 0:species] = start[...]
     load.wait()
 
-    flat = fv.reshape(SP * cx * YP, cz)
+    flat = fv.reshape(SP * cx * cy, cz)
     step = cfg["step"]
     wide = step * cz
     total = jnp.zeros((2 * SP, SP), F32)
     for x in range(cx):
         for g in range(cy // step):
-            cols = [flat[pl.ds(x * YP + g * step + k, SP, stride=cx * YP), :] for k in range(step)]
+            cols = [flat[pl.ds((g * step + k) * cx + x, SP, stride=cx * cy), :] for k in range(step)]
             high, low = split(jnp.concatenate(cols, axis=1))
             both = jnp.concatenate([high, low], axis=0)
             at = (x * (cy // step) + g) * wide
@@ -126,10 +130,9 @@
         return out
 
     packed = end_sum(start_sum(packed, b_sa, ns, sa, to_sa), b_sa, ns)
-    packed = end_sum(start_sum(packed, b_x, nx, mx, to_x), b_x, nx)
-    packed = end_sum(start_sum(packed, b_y, ny, my, to_y), b_y, ny)
+    packed = end_sum(start_sum(packed, b_p, nx * ny, gy, to_plane), b_p, nx * ny)
     copies = start_sum(packed, b_z, nz, gx, to_z)
-    w = zb[...].T[0:ranks]
+    w = wb[...]
     w = orth(orth(w, ranks), ranks)
     packed = end_sum(copies, b_z, nz)
 
@@ -181,8 +184,7 @@
         first1.append(send(core.at[there, :, hx:cx, 0:cy, :], mid1.at[:, :, my, 0:cy, :], to_y(d)))
     mid0[:, :, mx] = core[:, mx, 0:hx]
     mid1[:, :, my] = core[my, :, hx:cx]
-    zb[0:ranks] = w
-    basis_out[...] = zb[...].T[0:species, 0:ranks]
+    both_out[48:64] = w
     for copy in first0:
         copy.wait()
     second = []
@@ -218,24 +220,31 @@
         )
         return out.reshape(nx, YP, columns)
 
-    swaps = []
-    for y in range(ny):
+    hy = YP // 2
+    order = [lax.rem(my + t, ny) for t in range(1, ny)] + [my]
+    swaps, first0, first1 = [], [], []
+
+    def theirs(t):
+        y = order[t]
         gs[y] = gram_rows(y, 1 - sa)
         swaps.append(send(gs.at[y], gr.at[y], to_sa(1)))
-    for y in range(ny):
+
+    def ours(t):
+        y = order[t]
         mine = gram_rows(y, sa)
-        swaps[y].wait()
+        swaps[t].wait()
         go[y] = mine + gr[y]
-
-    hy = YP // 2
-    first0 = []
-    for d in range(1, nx):
-        there = lax.rem(mx + d, nx)
-        first0.append(send(go.at[:, there, 0:hy, :], r1a.at[d - 1], to_x(d)))
-    first1 = []
-    for d in range(1, ny):
-        there = lax.rem(my + d, ny)
-        first1.append(send(go.at[there, :, hy:YP, :], r1b.at[d - 1], to_y(d)))
+        for d in range(1, nx):
+            there = lax.rem(mx + d, nx)
+            first0.append(send(go.at[y, there, 0:hy, :], r1a.at[d - 1, y], to_x(d)))
+        if t < ny - 1:
+            first1.append(send(go.at[y, :, hy:YP, :], r1b.at[t], to_y(t + 1)))
+
+    theirs(0)
+    for t in range(1, ny):
+        theirs(t)
+        ours(t - 1)
+    ours(ny - 1)
     for copy in first0:
         copy.wait()
     out = go[:, mx, 0:hy, :]
@@ -267,21 +276,21 @@
         out = out + r2b[d - 1]
     hb[hy:YP, 0 : nz * YP] = out
 
-    fold = lax.broadcasted_iota(jnp.int32, (hy, LANES), 1) < LANES // 2
+    lane = lax.broadcasted_iota(jnp.int32, (16, LANES), 1)
     for g in range(nz):
         tile = (g * YP) // LANES
         at = g * YP - tile * LANES
         parts = []
-        for part in (hb[0:hy], hb[hy:YP]):
+        for part in (hb[0:16], hb[16:32], hb[32:48]):
             piece = part[:, tile * LANES : (tile + 1) * LANES]
             if at:
                 piece = pltpu.roll(piece, LANES - at, 1)
             if at + YP > LANES:
                 other = part[:, (tile + 1) * LANES : (tile + 2) * LANES]
-                where = lax.broadcasted_iota(jnp.int32, (hy, LANES), 1) < LANES - at
-                piece = jnp.where(where, piece, pltpu.roll(other, LANES - at, 1))
+                piece = jnp.where(lane < LANES - at, piece, pltpu.roll(other, LANES - at, 1))
             parts.append(piece)
-        pack[g] = jnp.where(fold, parts[0], pltpu.roll(parts[1], LANES // 2, 1))
+        moved = jnp.where(lane < 2 * cy, pltpu.roll(parts[1], cy, 1), pltpu.roll(parts[2], 2 * cy, 1))
+        pack[g] = jnp.where(lane < cy, parts[0], moved)
     last = []
     for d in range(1, nz):
         last.append(send(pack.at[lax.rem(gx + d, nz)], r3.at[d - 1], to_z(d)))
@@ -291,8 +300,14 @@
     for d in range(1, nz):
         out = out + r3[d - 1]
     out = out * (1.0 / cfg["terms"])
-    block_out[0:hy, :] = out[:, 0:cy]
-    block_out[hy:cy, :] = pltpu.roll(out, LANES // 2, 1)[0 : cy - hy, 0:cy]
+    both_out[0:16] = out
+    both_out[16:32] = pltpu.roll(out, LANES - cy, 1)
+    both_out[32:48] = pltpu.roll(out, LANES - 2 * cy, 1)
+
+
+def tail(species, cy, both, basis, block):
+    basis[...] = both[48:64, 0:species]
+    block[...] = both[0:cy, 0:cy]
 
 
 def on_device(cfg, field, start):
@@ -304,12 +319,11 @@
     hy = YP // 2
     hx = cx // 2
     cells = cx * cy * cz
-    copies = 1 + (nx - 1) + (ny - 1) + (nz - 1) + 2 * (nx + ny - 2) + ny + 2 * (nx + ny - 2) + nz - 1
+    copies = 1 + nx * ny - 1 + nz - 1 + 2 * (nx + ny - 2) + ny + ny * (nx - 1) + ny - 1 + nx + ny - 2 + nz - 1
     vmem = pltpu.VMEM
     scratch = [
-        vmem((SP, cx, YP, cz), F32), vmem((2 * SP, cells), BF16), vmem((SP, LANES), F32),
-        vmem((LANES, LANES), F32), vmem((2, 16, LANES), F32), vmem((nx, 16, LANES), F32),
-        vmem((ny, 16, LANES), F32), vmem((nz, 16, LANES), F32),
+        vmem((SP, cx * cy, cz), F32), vmem((2 * SP, cells), BF16), vmem((SP, LANES), F32),
+        vmem((LANES, LANES), F32), vmem((ranks, LANES), F32), vmem((2, 16, LANES), F32), vmem((nx * ny, 16, LANES), F32), vmem((nz, 16, LANES), F32),
         vmem((ny, nx, cx, YP, cz), F32), vmem((ny, hx, nx, YP, cz), F32),
         vmem((nx, hx, ny, YP, cz), F32), vmem((cx, ny, nx, YP, cz), F32),
         vmem((nz, 2, YP, cx * cz), BF16), vmem((nz, 2, YP, cx * cz), BF16),
@@ -317,23 +331,31 @@
         vmem((nx - 1, ny, hy, cols), F32), vmem((ny - 1, nx, hy, cols), F32),
         vmem((ny, hy, cols), F32), vmem((nx, hy, cols), F32),
         vmem((ny - 1, hy, cols), F32), vmem((nx - 1, hy, cols), F32),
-        vmem((YP, colsp), F32), vmem((nz, hy, LANES), F32), vmem((nz - 1, hy, LANES), F32),
+        vmem((YP, colsp), F32), vmem((nz, 16, LANES), F32), vmem((nz - 1, 16, LANES), F32),
         pltpu.SemaphoreType.DMA, pltpu.SemaphoreType.DMA((copies,)), pltpu.SemaphoreType.DMA((copies,)),
     ]
-    return pl.pallas_call(
+    both = pl.pallas_call(
         functools.partial(kernel, cfg),
-        out_shape=(
-            jax.ShapeDtypeStruct((species, ranks), F32),
-            jax.ShapeDtypeStruct((cy, cy), F32),
-        ),
+        out_shape=jax.ShapeDtypeStruct((64, LANES), F32),
         in_specs=[pl.BlockSpec(memory_space=pl.ANY), pl.BlockSpec(memory_space=vmem)],
-        out_specs=(pl.BlockSpec(memory_space=vmem), pl.BlockSpec(memory_space=vmem)),
+        out_specs=pl.BlockSpec(memory_space=vmem),
         scratch_shapes=scratch,
         compiler_params=pltpu.CompilerParams(
             collective_id=0, has_side_effects=True, vmem_limit_bytes=56 * 1024 * 1024
         ),
         name="tucker_step",
-    )(field, start)
+    )(field.transpose(0, 2, 1, 3).reshape(species, cx * cy, cz), start.T)
+    basis, block = pl.pallas_call(
+        functools.partial(tail, species, cy),
+        out_shape=(
+            jax.ShapeDtypeStruct((ranks, species), F32),
+            jax.ShapeDtypeStruct((cy, cy), F32),
+        ),
+        in_specs=[pl.BlockSpec(memory_space=vmem)],
+        out_specs=(pl.BlockSpec(memory_space=vmem), pl.BlockSpec(memory_space=vmem)),
+        name="parts",
+    )(both)
+    return basis.T, block
 
 
 def solution(mesh):
@@ -345,7 +367,7 @@
         species, cx, cy, cz = field.shape
         ranks = start.shape[1]
         total = cx * nz * cz * ns
-        full = dict(cfg, step=14 if cy % 14 == 0 else cy, cells=total * cy * n_plane, terms=ranks * total)
+        full = dict(cfg, cx=cx, cy=cy, step=14 if cy % 14 == 0 else cy, cells=total * cy * n_plane, terms=ranks * total)
         return on_device(full, field, start)
 
     return jax.shard_map(

time: 79.5 us -> 69.3 us (0.87)
  local copies, waits for them, and re-layouts: 7.91 us -> 0 us
  Pallas kernels: 70.6 us -> 68.4 us
    unnamed x3 -> x0, local copies, waits for them, and re-layouts: 6.51 us -> none
    pallas_call x1 -> x2, Pallas kernels: 70.6 us -> 68.4 us  [the longest x1 67 us: on_device(): pl.pallas_call(functools.partial(kernel, cfg), out_shape=jax.ShapeDtypeSt...]
    pallas_call x1 -> x0, local copies, waits for them, and re-layouts: 1.4 us -> none  [on_device(): pl.pallas_call(functools.partial(kernel, cfg), out_shape=(jax.ShapeDtypeS...]
where the time goes in v2:
time: 69.3 us; the launch traced here: 69 us
  Pallas kernels  68.4 us (99%)
    pallas_call x1, Pallas kernels, on_device(): pl.pallas_call(functools.partial(kernel, cfg), out_shape=jax.ShapeDtypeSt...  67 us

profile of v2, /device:TPU:8, one launch (start us, length us, event | category | flops | bytes accessed | tf_op | source)
XLA Modules:
  0.0 69.0 jit_solution(13180154583228217245)
XLA Ops:
  0.6 67.0 %tucker_step.1.both = f32[64,128]{1,0:T(8,128)} custom-call(f32[33,168,128]{2,1,0:T(8,128)} %bitcast.5, f32[16,33]{1,0:T(8,128)} %bitcast.6), custom_call_target="tpu_custom_call" | custom-call | tf_op jit(solution)/shard_map/tucker_step/pallas_call | solution.py:337
  67.7 1.4 %parts.1 = (f32[16,33]{1,0:T(8,128)}, f32[42,42]{1,0:T(8,128)}) custom-call(f32[64,128]{1,0:T(8,128)} %tucker_step.1.both), custom_call_target="tpu_custom_call" | custom-call | tf_op jit(solution)/shard_map/parts/pallas_call | solution.py:348

commit v3 on v2

--- a/solution.py
+++ b/solution.py
@@ -85,8 +85,13 @@
         copy.start()
         return copy
 
-    load = pltpu.make_async_copy(field, fv.at[0:species], load_sem)
-    load.start()
+    step = cfg["step"]
+    groups = cy // step
+    loads = []
+    for g in range(groups):
+        part = pl.ds(g * step * cx, step * cx)
+        loads.append(pltpu.make_async_copy(field.at[:, part], fv.at[0:species, part], load_sem.at[g]))
+        loads[g].start()
     barrier = pltpu.get_barrier_semaphore()
     peers = [to_sa(1)] + [to_plane(d) for d in range(1, nx * ny)]
     peers += [to_z(d) for d in range(1, nz)]
@@ -96,24 +101,28 @@
     ub[...] = jnp.zeros(ub.shape, F32)
     wb[...] = jnp.zeros(wb.shape, F32)
     wb[:, 0:species] = start[...]
-    load.wait()
 
     flat = fv.reshape(SP * cx * cy, cz)
-    step = cfg["step"]
     wide = step * cz
-    total = jnp.zeros((2 * SP, SP), F32)
-    for x in range(cx):
-        for g in range(cy // step):
+    total = jnp.zeros((2 * SP, 2 * SP), F32)
+    for g in range(groups):
+        loads[g].wait()
+        for x in range(cx):
             cols = [flat[pl.ds((g * step + k) * cx + x, SP, stride=cx * cy), :] for k in range(step)]
             high, low = split(jnp.concatenate(cols, axis=1))
             both = jnp.concatenate([high, low], axis=0)
-            at = (x * (cy // step) + g) * wide
+            at = (x * groups + g) * wide
             hl[:, at : at + wide] = both
-            total = total + lax.dot_general(both, high, NT, preferred_element_type=F32)
-    ub[0:SP, 0:SP] = total[0:SP] * 0.5 + total[SP:]
-    lane = lax.broadcasted_iota(jnp.int32, (SP, LANES), 1)
-    half = ub[...]
-    packed = half[0:16] + pltpu.roll(half[16:32], 42, 1) + pltpu.roll(half[32:48], 84, 1)
+            total = total + lax.dot_general(both, both, NT, preferred_element_type=F32)
+    ub[:, 0 : 2 * SP] = total
+    full = ub[0:SP] + ub[SP:] + pltpu.roll(ub[0:SP], LANES - SP, 1)
+    lane = lax.broadcasted_iota(jnp.int32, (8, LANES), 1)
+    starts = range(0, species, 8)
+    shifts = [sum(species - a for a in starts[:b]) - at for b, at in enumerate(starts)]
+    packed = jnp.zeros((8, LANES), F32)
+    for at, shift in zip(starts, shifts):
+        rows = jnp.where((lane >= at) & (lane < species), full[at : at + 8], 0.0)
+        packed = packed + (pltpu.roll(rows, shift, 1) if shift else rows)
 
     pl.semaphore_wait(barrier, len(peers))
 
@@ -138,15 +147,14 @@
 
     scale = 1.0 / cfg["cells"]
     packed = packed * scale
-    ub[0:16] = packed
-    ub[16:32] = pltpu.roll(packed, LANES - 42, 1)
-    ub[32:48] = pltpu.roll(packed, LANES - 84, 1)
-    srow = lax.broadcasted_iota(jnp.int32, (SP, LANES), 0)
-    half = jnp.where((lane < species) & (srow < species), ub[...], 0.0)
     zb[...] = jnp.zeros(zb.shape, F32)
-    zb[0:SP] = half
-    half = zb[...]
-    gram = half + half.T
+    for at, shift in zip(starts, shifts):
+        rows = pltpu.roll(packed, LANES - shift, 1) if shift else packed
+        zb[at : at + 8] = jnp.where((lane >= at) & (lane < species), rows, 0.0)
+    upper = zb[...]
+    row = lax.broadcasted_iota(jnp.int32, zb.shape, 0)
+    column = lax.broadcasted_iota(jnp.int32, zb.shape, 1)
+    gram = upper + jnp.where(column >= (row & ~7) + 8, upper, 0.0).T
 
     def round_(i, w):
         w = jnp.dot(w, gram, precision=HIGH, preferred_element_type=F32)
@@ -160,8 +168,8 @@
     cflat = core.reshape(ranks * cx * YP, cz)
 
     def project(x):
-        for g in range(cy // step):
-            at = (x * (cy // step) + g) * wide
+        for g in range(groups):
+            at = (x * groups + g) * wide
             out = jnp.dot(lhs, hl[:, at : at + wide], preferred_element_type=F32)
             out = out[0:ranks] + out[ranks:]
             for k in range(step):
@@ -170,39 +178,45 @@
                 )
 
     hx = cx // 2
-    for x in range(hx):
+    firsts = {}
+    for a in range(hx):
+        project(a)
+        firsts[a] = []
+        for d in range(1, nx):
+            there = lax.rem(mx + d, nx)
+            firsts[a].append(send(core.at[:, there, a, 0:cy], mid0.at[a, :, mx, 0:cy], to_x(d)))
+        x = hx + a
         project(x)
-    first0 = []
-    for d in range(1, nx):
-        there = lax.rem(mx + d, nx)
-        first0.append(send(core.at[:, there, 0:hx, 0:cy, :], mid0.at[:, :, mx, 0:cy, :], to_x(d)))
-    for x in range(hx, cx):
-        project(x)
-    first1 = []
-    for d in range(1, ny):
-        there = lax.rem(my + d, ny)
-        first1.append(send(core.at[there, :, hx:cx, 0:cy, :], mid1.at[:, :, my, 0:cy, :], to_y(d)))
-    mid0[:, :, mx] = core[:, mx, 0:hx]
-    mid1[:, :, my] = core[my, :, hx:cx]
+        firsts[x] = []
+        for d in range(1, ny):
+            there = lax.rem(my + d, ny)
+            firsts[x].append(send(core.at[there, :, x, 0:cy], mid1.at[a, :, my, 0:cy], to_y(d)))
+    for a in range(hx):
+        mid0[a, :, mx] = core[:, mx, a]
+        mid1[a, :, my] = core[my, :, hx + a]
     both_out[48:64] = w
-    for copy in first0:
-        copy.wait()
-    second = []
-    for d in range(1, ny):
-        there = lax.rem(my + d, ny)
-        second.append(send(mid0.at[there, :, :, 0:cy, :], recv.at[0:hx, my, :, 0:cy, :], to_y(d)))
-    recv[0:hx, my] = mid0[my]
-    for copy in first1:
-        copy.wait()
-    for d in range(1, nx):
-        there = lax.rem(mx + d, nx)
-        second.append(send(mid1.at[there, :, :, 0:cy, :], recv.at[hx:cx, :, mx, 0:cy, :], to_x(d)))
-    recv[hx:cx, :, mx] = mid1[mx]
-    for copy in second:
-        copy.wait()
+    seconds = {}
+    for a in range(hx):
+        for copy in firsts[a]:
+            copy.wait()
+        seconds[a] = []
+        for d in range(1, ny):
+            there = lax.rem(my + d, ny)
+            seconds[a].append(send(mid0.at[a, there, :, 0:cy], recv.at[a, my, :, 0:cy], to_y(d)))
+        recv[a, my] = mid0[a, my]
+        x = hx + a
+        for copy in firsts[x]:
+            copy.wait()
+        seconds[x] = []
+        for d in range(1, nx):
+            there = lax.rem(mx + d, nx)
+            seconds[x].append(send(mid1.at[a, there, :, 0:cy], recv.at[x, :, mx, 0:cy], to_x(d)))
+        recv[x, :, mx] = mid1[a, mx]
 
     rows = ny * nx * YP
-    for x in range(cx):
+    for x in [k for a in range(hx) for k in (a, hx + a)]:
+        for copy in seconds[x]:
+            copy.wait()
         high, low = split(recv[x].reshape(rows, cz))
         ah[:, :, :, x * cz : (x + 1) * cz] = high.reshape(nz, ns, YP, cz)
         al[:, :, :, x * cz : (x + 1) * cz] = low.reshape(nz, ns, YP, cz)
@@ -222,7 +236,7 @@
 
     hy = YP // 2
     order = [lax.rem(my + t, ny) for t in range(1, ny)] + [my]
-    swaps, first0, first1 = [], [], []
+    swaps, first0, first1 = [], {}, {}
 
     def theirs(t):
         y = order[t]
@@ -236,45 +250,50 @@
         go[y] = mine + gr[y]
         for d in range(1, nx):
             there = lax.rem(mx + d, nx)
-            first0.append(send(go.at[y, there, 0:hy, :], r1a.at[d - 1, y], to_x(d)))
+            first0[t, d] = send(go.at[y, there, 0:hy, :], r1a.at[d - 1, y], to_x(d))
         if t < ny - 1:
-            first1.append(send(go.at[y, :, hy:YP, :], r1b.at[t], to_y(t + 1)))
+            for d in list(range(1, nx)) + [0]:
+                there = lax.rem(mx + d, nx)
+                first1[t, d] = send(go.at[y, there, hy:YP, :], r1b.at[t, there], to_y(t + 1))
 
     theirs(0)
     for t in range(1, ny):
         theirs(t)
         ours(t - 1)
     ours(ny - 1)
-    for copy in first0:
-        copy.wait()
-    out = go[:, mx, 0:hy, :]
-    for d in range(1, nx):
-        out = out + r1a[d - 1]
-    t0[...] = out
-    second0 = []
-    for d in range(1, ny):
-        second0.append(send(t0.at[lax.rem(my + d, ny)], r2a.at[d - 1], to_y(d)))
-    for copy in first1:
-        copy.wait()
-    out = go[my, :, hy:YP, :]
-    for d in range(1, ny):
-        out = out + r1b[d - 1]
-    t1[...] = out
-    second1 = []
-    for d in range(1, nx):
-        second1.append(send(t1.at[lax.rem(mx + d, nx)], r2b.at[d - 1], to_x(d)))
-    for copy in second0:
-        copy.wait()
-    out = t0[my]
-    for d in range(1, ny):
-        out = out + r2a[d - 1]
-    hb[0:hy, 0 : nz * YP] = out
-    for copy in second1:
-        copy.wait()
-    out = t1[mx]
-    for d in range(1, nx):
-        out = out + r2b[d - 1]
-    hb[hy:YP, 0 : nz * YP] = out
+    def sum0(t):
+        y = order[t]
+        out = go[y, mx, 0:hy, :]
+        for d in range(1, nx):
+            first0[t, d].wait()
+            out = out + r1a[d - 1, y]
+        return out
+
+    def sum1(d):
+        there = lax.rem(mx + d, nx)
+        out = go[my, there, hy:YP, :]
+        for t in range(ny - 1):
+            first1[t, d].wait()
+            out = out + r1b[t, there]
+        return out
+
+    second0, second1 = [], []
+    for k in range(max(nx, ny) - 1):
+        if k < ny - 1:
+            t0[k] = sum0(k)
+            second0.append(send(t0.at[k], r2a.at[k], to_y(k + 1)))
+        if k < nx - 1:
+            t1[k] = sum1(k + 1)
+            second1.append(send(t1.at[k], r2b.at[k], to_x(k + 1)))
+    out0, out1 = sum0(ny - 1), sum1(0)
+    for k in range(ny - 1):
+        second0[k].wait()
+        out0 = out0 + r2a[k]
+    for k in range(nx - 1):
+        second1[k].wait()
+        out1 = out1 + r2b[k]
+    hb[0:hy, 0 : nz * YP] = out0
+    hb[hy:YP, 0 : nz * YP] = out1
 
     lane = lax.broadcasted_iota(jnp.int32, (16, LANES), 1)
     for g in range(nz):
@@ -319,20 +338,21 @@
     hy = YP // 2
     hx = cx // 2
     cells = cx * cy * cz
-    copies = 1 + nx * ny - 1 + nz - 1 + 2 * (nx + ny - 2) + ny + ny * (nx - 1) + ny - 1 + nx + ny - 2 + nz - 1
+    ring = nx + ny - 2
+    copies = 1 + nx * ny - 1 + nz - 1 + 2 * hx * ring + ny + 2 * nx * ny - nx - ny + nx * (ny - 1) + ring + nz
     vmem = pltpu.VMEM
     scratch = [
-        vmem((SP, cx * cy, cz), F32), vmem((2 * SP, cells), BF16), vmem((SP, LANES), F32),
-        vmem((LANES, LANES), F32), vmem((ranks, LANES), F32), vmem((2, 16, LANES), F32), vmem((nx * ny, 16, LANES), F32), vmem((nz, 16, LANES), F32),
-        vmem((ny, nx, cx, YP, cz), F32), vmem((ny, hx, nx, YP, cz), F32),
-        vmem((nx, hx, ny, YP, cz), F32), vmem((cx, ny, nx, YP, cz), F32),
+        vmem((SP, cx * cy, cz), F32), vmem((2 * SP, cells), BF16), vmem((2 * SP, LANES), F32),
+        vmem((LANES, LANES), F32), vmem((ranks, LANES), F32), vmem((2, 8, LANES), F32), vmem((nx * ny, 8, LANES), F32), vmem((nz, 8, LANES), F32),
+        vmem((ny, nx, cx, YP, cz), F32), vmem((hx, ny, nx, YP, cz), F32),
+        vmem((hx, nx, ny, YP, cz), F32), vmem((cx, ny, nx, YP, cz), F32),
         vmem((nz, 2, YP, cx * cz), BF16), vmem((nz, 2, YP, cx * cz), BF16),
         vmem((ny, nx, YP, cols), F32), vmem((ny, nx, YP, cols), F32), vmem((ny, nx, YP, cols), F32),
         vmem((nx - 1, ny, hy, cols), F32), vmem((ny - 1, nx, hy, cols), F32),
-        vmem((ny, hy, cols), F32), vmem((nx, hy, cols), F32),
+        vmem((ny - 1, hy, cols), F32), vmem((nx - 1, hy, cols), F32),
         vmem((ny - 1, hy, cols), F32), vmem((nx - 1, hy, cols), F32),
         vmem((YP, colsp), F32), vmem((nz, 16, LANES), F32), vmem((nz - 1, 16, LANES), F32),
-        pltpu.SemaphoreType.DMA, pltpu.SemaphoreType.DMA((copies,)), pltpu.SemaphoreType.DMA((copies,)),
+        pltpu.SemaphoreType.DMA((cfg["cy"] // cfg["step"],)), pltpu.SemaphoreType.DMA((copies,)), pltpu.SemaphoreType.DMA((copies,)),
     ]
     both = pl.pallas_call(
         functools.partial(kernel, cfg),

time: 69.3 us -> 64.8 us (0.935)
  Pallas kernels: 68.4 us -> 63.9 us
    pallas_call x1, Pallas kernels: 67 us -> 62.6 us  [on_device(): pl.pallas_call(functools.partial(kernel, cfg), out_shape=jax.ShapeDtypeSt...]
where the time goes in v3:
time: 64.8 us; the launch traced here: 64.6 us
  Pallas kernels  63.9 us (99%)
    pallas_call x1, Pallas kernels, on_device(): pl.pallas_call(functools.partial(kernel, cfg), out_shape=jax.ShapeDtypeSt...  62.6 us
    pallas_call x1, Pallas kernels, on_device(): pl.pallas_call(functools.partial(tail, species, cy), out_shape=(jax.Shape...  1.37 us

profile of v3, /device:TPU:8, one launch (start us, length us, event | category | flops | bytes accessed | tf_op | source)
XLA Modules:
  0.0 64.6 jit_solution(16077548665872004387)
XLA Ops:
  0.6 62.6 %tucker_step.1.both = f32[64,128]{1,0:T(8,128)} custom-call(f32[33,168,128]{2,1,0:T(8,128)} %bitcast.5, f32[16,33]{1,0:T(8,128)} %bitcast.6), custom_call_target="tpu_custom_call" | custom-call | tf_op jit(solution)/shard_map/tucker_step/pallas_call | solution.py:357
  63.2 1.4 %parts.1 = (f32[16,33]{1,0:T(8,128)}, f32[42,42]{1,0:T(8,128)}) custom-call(f32[64,128]{1,0:T(8,128)} %tucker_step.1.both), custom_call_target="tpu_custom_call" | custom-call | tf_op jit(solution)/shard_map/parts/pallas_call | solution.py:368

commit v4 on v3

--- a/solution.py
+++ b/solution.py
@@ -49,7 +49,7 @@
 
 
 def kernel(cfg, field, start, both_out, fv, hl, ub, zb, wb, b_sa, b_p, b_z,
-           core, mid0, mid1, recv, ah, al, gs, go, gr, r1a, r1b, t0, t1, r2a, r2b, hb, pack, r3,
+           ft, raw, own_a, cd, ca, recv_d, recv_a, ah, al, gs, go, gr, r1a, r1b, t0, t1, r2a, r2b, hb, pack, r3,
            load_sem, ssem, rsem):
     nx, ny, nz, ns = cfg["nx"], cfg["ny"], cfg["nz"], 2
     species, cz = field.shape[0], field.shape[2]
@@ -69,6 +69,17 @@
 
     def to_plane(d):
         return {"gy": lax.rem(my + d // nx, ny) * nx + lax.rem(mx + d % nx, nx)}
+
+    p = (1 - sa) * mx + sa * my
+    q = (1 - sa) * my + sa * mx
+
+    def to_first(d):
+        there = lax.rem(p + d, nx)
+        return {"gy": (1 - sa) * (q * nx + there) + sa * (there * nx + q)}
+
+    def to_second(d):
+        there = lax.rem(q + d, ny)
+        return {"gy": (1 - sa) * (there * nx + p) + sa * (p * nx + there)}
 
     def to_z(d):
         return {"gx": lax.rem(gx + d, nz)}
@@ -85,11 +96,11 @@
         copy.start()
         return copy
 
-    step = cfg["step"]
-    groups = cy // step
+    hy = YP // 2
+    groups = [(0, hy // 2), (hy // 2, hy // 2), (hy, cy - hy)]
     loads = []
-    for g in range(groups):
-        part = pl.ds(g * step * cx, step * cx)
+    for g, (y0, n) in enumerate(groups):
+        part = pl.ds(y0 * cx, n * cx)
         loads.append(pltpu.make_async_copy(field.at[:, part], fv.at[0:species, part], load_sem.at[g]))
         loads[g].start()
     barrier = pltpu.get_barrier_semaphore()
@@ -103,16 +114,19 @@
     wb[:, 0:species] = start[...]
 
     flat = fv.reshape(SP * cx * cy, cz)
-    wide = step * cz
     total = jnp.zeros((2 * SP, 2 * SP), F32)
-    for g in range(groups):
+    wide = (cy - hy) * cz
+    for g, (y0, n) in enumerate(groups):
         loads[g].wait()
         for x in range(cx):
-            cols = [flat[pl.ds((g * step + k) * cx + x, SP, stride=cx * cy), :] for k in range(step)]
+            cols = [flat[pl.ds((y0 + k) * cx + x, SP, stride=cx * cy), :] for k in range(n)]
+            if y0 < hy:
+                for k in range(n):
+                    ft[x, y0 + k] = cols[k]
             high, low = split(jnp.concatenate(cols, axis=1))
             both = jnp.concatenate([high, low], axis=0)
-            at = (x * groups + g) * wide
-            hl[:, at : at + wide] = both
+            if y0 >= hy:
+                hl[:, x * wide : (x + 1) * wide] = both
             total = total + lax.dot_general(both, both, NT, preferred_element_type=F32)
     ub[:, 0 : 2 * SP] = total
     full = ub[0:SP] + ub[SP:] + pltpu.roll(ub[0:SP], LANES - SP, 1)
@@ -141,6 +155,10 @@
     packed = end_sum(start_sum(packed, b_sa, ns, sa, to_sa), b_sa, ns)
     packed = end_sum(start_sum(packed, b_p, nx * ny, gy, to_plane), b_p, nx * ny)
     copies = start_sum(packed, b_z, nz, gx, to_z)
+    bulk = {}
+    for d in range(1, nx):
+        there = lax.rem(p + d, nx)
+        bulk[d] = send(ft.at[there, :, 0:species], raw.at[d - 1, :, 0:species], to_first(d))
     w = wb[...]
     w = orth(orth(w, ranks), ranks)
     packed = end_sum(copies, b_z, nz)
@@ -165,62 +183,75 @@
     whigh = w.astype(BF16).astype(F32)
     lhs = jnp.concatenate([whigh + pltpu.roll(whigh, SP, 1), w - whigh], axis=0).astype(BF16)
     lhs = lhs[:, 0 : 2 * SP]
-    cflat = core.reshape(ranks * cx * YP, cz)
-
-    def project(x):
-        for g in range(groups):
-            at = (x * groups + g) * wide
-            out = jnp.dot(lhs, hl[:, at : at + wide], preferred_element_type=F32)
-            out = out[0:ranks] + out[ranks:]
-            for k in range(step):
-                cflat[pl.ds(x * YP + g * step + k, ranks, stride=cx * YP), :] = (
-                    out[:, k * cz : (k + 1) * cz]
-                )
-
-    hx = cx // 2
-    firsts = {}
-    for a in range(hx):
-        project(a)
-        firsts[a] = []
-        for d in range(1, nx):
-            there = lax.rem(mx + d, nx)
-            firsts[a].append(send(core.at[:, there, a, 0:cy], mid0.at[a, :, mx, 0:cy], to_x(d)))
-        x = hx + a
-        project(x)
-        firsts[x] = []
-        for d in range(1, ny):
-            there = lax.rem(my + d, ny)
-            firsts[x].append(send(core.at[there, :, x, 0:cy], mid1.at[a, :, my, 0:cy], to_y(d)))
-    for a in range(hx):
-        mid0[a, :, mx] = core[:, mx, a]
-        mid1[a, :, my] = core[my, :, hx + a]
+    rg = ranks // ny
+    aflat = own_a.reshape(ranks * cx * hy, cz)
+    dflat = cd.reshape(ranks * nx * hy, cz)
+    cd4, ca4 = cd.reshape(ny, rg, nx, hy, cz), ca.reshape(ny, rg, nx, hy, cz)
+    srow = lax.broadcasted_iota(jnp.int32, (SP, cz), 0)
+
+    def project(both):
+        out = jnp.dot(lhs, both, preferred_element_type=F32)
+        return out[0:ranks] + out[ranks:]
+
+    def project_raw(d):
+        n = hy // 2
+        for h in range(0, hy, n):
+            if d:
+                tiles = [jnp.where(srow < species, raw[d - 1, h + k], 0.0) for k in range(n)]
+            else:
+                tiles = [ft[p, h + k] for k in range(n)]
+            high, low = split(jnp.concatenate(tiles, axis=1))
+            out = project(jnp.concatenate([high, low], axis=0))
+            for k in range(n):
+                dflat[pl.ds(d * hy + h + k, ranks, stride=nx * hy), :] = out[:, k * cz : (k + 1) * cz]
+
+    low_rows = cy - hy
+    for x in range(cx):
+        out = project(hl[:, x * wide : (x + 1) * wide])
+        for k in range(low_rows):
+            aflat[pl.ds(x * hy + k, ranks, stride=cx * hy), :] = out[:, k * cz : (k + 1) * cz]
+    firsts = []
+    for d in range(1, nx):
+        there = lax.rem(p + d, nx)
+        firsts.append(send(own_a.at[:, there, 0:low_rows], ca.at[:, d, 0:low_rows], to_first(d)))
+    seconds = []
+    for d in [0] + sorted(range(1, nx), key=lambda d: min(d, nx - d)):
+        if d:
+            bulk[d].wait()
+        project_raw(d)
+        for e in range(1, ny):
+            there = lax.rem(q + e, ny)
+            seconds.append(send(cd4.at[there, :, d], recv_d.at[e - 1, :, d], to_second(e)))
+    ca[:, 0] = own_a[:, p]
     both_out[48:64] = w
-    seconds = {}
-    for a in range(hx):
-        for copy in firsts[a]:
-            copy.wait()
-        seconds[a] = []
-        for d in range(1, ny):
-            there = lax.rem(my + d, ny)
-            seconds[a].append(send(mid0.at[a, there, :, 0:cy], recv.at[a, my, :, 0:cy], to_y(d)))
-        recv[a, my] = mid0[a, my]
-        x = hx + a
-        for copy in firsts[x]:
-            copy.wait()
-        seconds[x] = []
-        for d in range(1, nx):
-            there = lax.rem(mx + d, nx)
-            seconds[x].append(send(mid1.at[a, there, :, 0:cy], recv.at[x, :, mx, 0:cy], to_x(d)))
-        recv[x, :, mx] = mid1[a, mx]
-
-    rows = ny * nx * YP
-    for x in [k for a in range(hx) for k in (a, hx + a)]:
-        for copy in seconds[x]:
-            copy.wait()
-        high, low = split(recv[x].reshape(rows, cz))
-        ah[:, :, :, x * cz : (x + 1) * cz] = high.reshape(nz, ns, YP, cz)
-        al[:, :, :, x * cz : (x + 1) * cz] = low.reshape(nz, ns, YP, cz)
-    depth = cx * cz
+    for copy in firsts:
+        copy.wait()
+    for e in range(1, ny):
+        there = lax.rem(q + e, ny)
+        seconds.append(
+            send(ca4.at[there, :, :, 0:low_rows], recv_a.at[e - 1, :, :, 0:low_rows], to_second(e))
+        )
+
+    def place(e, d):
+        above, below = lax.rem(q + ny - e, ny), lax.rem(p + nx - d, nx)
+        block = (1 - sa) * (above * nx + below) + sa * (below * nx + above)
+        parts = []
+        for r in range(rg):
+            top = recv_d[e - 1, r, d] if e else cd4[q, r, d]
+            end = recv_a[e - 1, r, d] if e else ca4[q, r, d]
+            parts.append(jnp.concatenate([top, end], axis=0))
+        high, low = split(jnp.concatenate(parts, axis=1))
+        ah[block // ns, lax.rem(block, ns)] = high
+        al[block // ns, lax.rem(block, ns)] = low
+
+    for d in range(nx):
+        place(0, d)
+    for copy in seconds:
+        copy.wait()
+    for e in range(1, ny):
+        for d in range(nx):
+            place(e, d)
+    depth = rg * cz
     columns = nz * YP
     lrows = ah.reshape(ny, nx * YP, depth), al.reshape(ny, nx * YP, depth)
 
@@ -234,7 +265,6 @@
         )
         return out.reshape(nx, YP, columns)
 
-    hy = YP // 2
     order = [lax.rem(my + t, ny) for t in range(1, ny)] + [my]
     swaps, first0, first1 = [], {}, {}
 
@@ -336,23 +366,23 @@
     cols = nz * YP
     colsp = -(-cols // LANES) * LANES
     hy = YP // 2
-    hx = cx // 2
-    cells = cx * cy * cz
+    depth = ranks // ny * cz
     ring = nx + ny - 2
-    copies = 1 + nx * ny - 1 + nz - 1 + 2 * hx * ring + ny + 2 * nx * ny - nx - ny + nx * (ny - 1) + ring + nz
+    copies = 1 + nx * ny - 1 + nz - 1 + nx + nx + nx * ny + ny + ny + 2 * nx * ny - nx - ny + nx * (ny - 1) + ring + nz
     vmem = pltpu.VMEM
     scratch = [
-        vmem((SP, cx * cy, cz), F32), vmem((2 * SP, cells), BF16), vmem((2 * SP, LANES), F32),
+        vmem((SP, cx * cy, cz), F32), vmem((2 * SP, cx * (cy - hy) * cz), BF16), vmem((2 * SP, LANES), F32),
         vmem((LANES, LANES), F32), vmem((ranks, LANES), F32), vmem((2, 8, LANES), F32), vmem((nx * ny, 8, LANES), F32), vmem((nz, 8, LANES), F32),
-        vmem((ny, nx, cx, YP, cz), F32), vmem((hx, ny, nx, YP, cz), F32),
-        vmem((hx, nx, ny, YP, cz), F32), vmem((cx, ny, nx, YP, cz), F32),
-        vmem((nz, 2, YP, cx * cz), BF16), vmem((nz, 2, YP, cx * cz), BF16),
+        vmem((cx, hy, SP, cz), F32), vmem((nx - 1, hy, SP, cz), F32),
+        vmem((ranks, cx, hy, cz), F32), vmem((ranks, nx, hy, cz), F32), vmem((ranks, nx, hy, cz), F32),
+        vmem((ny - 1, ranks // ny, nx, hy, cz), F32), vmem((ny - 1, ranks // ny, nx, hy, cz), F32),
+        vmem((nz, 2, YP, depth), BF16), vmem((nz, 2, YP, depth), BF16),
         vmem((ny, nx, YP, cols), F32), vmem((ny, nx, YP, cols), F32), vmem((ny, nx, YP, cols), F32),
         vmem((nx - 1, ny, hy, cols), F32), vmem((ny - 1, nx, hy, cols), F32),
         vmem((ny - 1, hy, cols), F32), vmem((nx - 1, hy, cols), F32),
         vmem((ny - 1, hy, cols), F32), vmem((nx - 1, hy, cols), F32),
         vmem((YP, colsp), F32), vmem((nz, 16, LANES), F32), vmem((nz - 1, 16, LANES), F32),
-        pltpu.SemaphoreType.DMA((cfg["cy"] // cfg["step"],)), pltpu.SemaphoreType.DMA((copies,)), pltpu.SemaphoreType.DMA((copies,)),
+        pltpu.SemaphoreType.DMA((3,)), pltpu.SemaphoreType.DMA((copies,)), pltpu.SemaphoreType.DMA((copies,)),
     ]
     both = pl.pallas_call(
         functools.partial(kernel, cfg),
@@ -387,7 +417,7 @@
         species, cx, cy, cz = field.shape
         ranks = start.shape[1]
         total = cx * nz * cz * ns
-        full = dict(cfg, cx=cx, cy=cy, step=14 if cy % 14 == 0 else cy, cells=total * cy * n_plane, terms=ranks * total)
+        full = dict(cfg, cx=cx, cy=cy, cells=total * cy * n_plane, terms=ranks * total)
         return on_device(full, field, start)
 
     return jax.shard_map(

time: 64.8 us -> 68.5 us (1.057)
  Pallas kernels: 63.9 us -> 67.3 us
    pallas_call x1, Pallas kernels: 62.6 us -> 65.9 us  [on_device(): pl.pallas_call(functools.partial(kernel, cfg), out_shape=jax.ShapeDtypeSt...]
where the time goes in v4:
time: 68.5 us; the launch traced here: 67.9 us
  Pallas kernels  67.3 us (98%)
    pallas_call x1, Pallas kernels, on_device(): pl.pallas_call(functools.partial(kernel, cfg), out_shape=jax.ShapeDtypeSt...  65.9 us
    pallas_call x1, Pallas kernels, on_device(): pl.pallas_call(functools.partial(tail, species, cy), out_shape=(jax.Shape...  1.37 us

profile of v4, /device:TPU:8, one launch (start us, length us, event | category | flops | bytes accessed | tf_op | source)
XLA Modules:
  0.0 67.9 jit_solution(6475244917945454999)
XLA Ops:
  0.6 65.9 %tucker_step.1.both = f32[64,128]{1,0:T(8,128)} custom-call(f32[33,168,128]{2,1,0:T(8,128)} %bitcast.5, f32[16,33]{1,0:T(8,128)} %bitcast.6), custom_call_target="tpu_custom_call" | custom-call | tf_op jit(solution)/shard_map/tucker_step/pallas_call | solution.py:387
  66.6 1.4 %parts.1 = (f32[16,33]{1,0:T(8,128)}, f32[42,42]{1,0:T(8,128)}) custom-call(f32[64,128]{1,0:T(8,128)} %tucker_step.1.both), custom_call_target="tpu_custom_call" | custom-call | tf_op jit(solution)/shard_map/parts/pallas_call | solution.py:398

commit v5 on v3

--- a/solution.py
+++ b/solution.py
@@ -15,6 +15,7 @@
 LANES = 128
 SP = 48
 YP = 48
+GROUP = 40
 NT = (((1,), (1,)), ((), ()))
 
 
@@ -25,14 +26,13 @@
 
 def orth(w, ranks):
     products = (w[:, None, :] * w[None, :, :]).reshape(ranks * ranks, LANES)
-    first, rest = split(products)
-    second, third = split(products - first.astype(F32))
+    lane = lax.broadcasted_iota(jnp.int32, products.shape, 1)
+    first = products.astype(BF16).astype(F32)
+    rest = products - first
+    second = rest.astype(BF16).astype(F32)
+    pieces = jnp.where(lane < GROUP, first, jnp.where(lane < 2 * GROUP, second, rest - second))
     ones = jnp.ones((LANES, LANES), BF16)
-    inner = (
-        jnp.dot(first, ones, preferred_element_type=F32)
-        + jnp.dot(second, ones, preferred_element_type=F32)
-        + jnp.dot(third, ones, preferred_element_type=F32)
-    )
+    inner = jnp.dot(pieces.astype(BF16), ones, preferred_element_type=F32)
     lines = [inner[i * ranks : (i + 1) * ranks] for i in range(ranks)]
     row = lax.broadcasted_iota(jnp.int32, (ranks, LANES), 0)
     pivots = jnp.ones((ranks, LANES), F32)
@@ -100,7 +100,8 @@
     fv[species:SP] = jnp.zeros((SP - species, cx * cy, cz), F32)
     ub[...] = jnp.zeros(ub.shape, F32)
     wb[...] = jnp.zeros(wb.shape, F32)
-    wb[:, 0:species] = start[...]
+    for c in range(3):
+        wb[:, c * GROUP : c * GROUP + species] = start[...]
 
     flat = fv.reshape(SP * cx * cy, cz)
     wide = step * cz
@@ -155,6 +156,7 @@
     row = lax.broadcasted_iota(jnp.int32, zb.shape, 0)
     column = lax.broadcasted_iota(jnp.int32, zb.shape, 1)
     gram = upper + jnp.where(column >= (row & ~7) + 8, upper, 0.0).T
+    gram = gram + pltpu.roll(gram, GROUP, 1) + pltpu.roll(gram, 2 * GROUP, 1)
 
     def round_(i, w):
         w = jnp.dot(w, gram, precision=HIGH, preferred_element_type=F32)
@@ -162,6 +164,7 @@
 
     w = lax.fori_loop(0, ITERS, round_, w)
 
+    w = jnp.where(lax.broadcasted_iota(jnp.int32, w.shape, 1) < species, w, 0.0)
     whigh = w.astype(BF16).astype(F32)
     lhs = jnp.concatenate([whigh + pltpu.roll(whigh, SP, 1), w - whigh], axis=0).astype(BF16)
     lhs = lhs[:, 0 : 2 * SP]
@@ -214,19 +217,23 @@
         recv[x, :, mx] = mid1[a, mx]
 
     rows = ny * nx * YP
-    for x in [k for a in range(hx) for k in (a, hx + a)]:
-        for copy in seconds[x]:
-            copy.wait()
-        high, low = split(recv[x].reshape(rows, cz))
-        ah[:, :, :, x * cz : (x + 1) * cz] = high.reshape(nz, ns, YP, cz)
-        al[:, :, :, x * cz : (x + 1) * cz] = low.reshape(nz, ns, YP, cz)
+    columns = nz * YP
     depth = cx * cz
-    columns = nz * YP
     lrows = ah.reshape(ny, nx * YP, depth), al.reshape(ny, nx * YP, depth)
 
-    def gram_rows(y, side):
-        lh, ll = lrows[0][y], lrows[1][y]
-        rh, rl = ah[:, side].reshape(columns, depth), al[:, side].reshape(columns, depth)
+    def arrive(a):
+        for at, x in ((2 * a, a), (2 * a + 1, hx + a)):
+            for copy in seconds[x]:
+                copy.wait()
+            high, low = split(recv[x].reshape(rows, cz))
+            ah[:, :, :, at * cz : (at + 1) * cz] = high.reshape(nz, ns, YP, cz)
+            al[:, :, :, at * cz : (at + 1) * cz] = low.reshape(nz, ns, YP, cz)
+
+    def gram_rows(y, side, a):
+        part = slice(2 * a * cz, 2 * (a + 1) * cz)
+        lh, ll = lrows[0][y, :, part], lrows[1][y, :, part]
+        rh = ah[:, side, :, part].reshape(columns, 2 * cz)
+        rl = al[:, side, :, part].reshape(columns, 2 * cz)
         out = (
             lax.dot_general(lh, rh, NT, preferred_element_type=F32)
             + lax.dot_general(lh, rl, NT, preferred_element_type=F32)
@@ -234,18 +241,26 @@
         )
         return out.reshape(nx, YP, columns)
 
+    for a in range(hx - 1):
+        arrive(a)
+        for y in range(ny):
+            for side, sums in ((1 - sa, gs), (sa, go)):
+                out = gram_rows(y, side, a)
+                sums[y] = out if a == 0 else sums[y] + out
+    arrive(hx - 1)
+
     hy = YP // 2
     order = [lax.rem(my + t, ny) for t in range(1, ny)] + [my]
     swaps, first0, first1 = [], {}, {}
 
     def theirs(t):
         y = order[t]
-        gs[y] = gram_rows(y, 1 - sa)
+        gs[y] = gs[y] + gram_rows(y, 1 - sa, hx - 1)
         swaps.append(send(gs.at[y], gr.at[y], to_sa(1)))
 
     def ours(t):
         y = order[t]
-        mine = gram_rows(y, sa)
+        mine = go[y] + gram_rows(y, sa, hx - 1)
         swaps[t].wait()
         go[y] = mine + gr[y]
         for d in range(1, nx):

time: 64.8 us -> 64.4 us (level)
  Pallas kernels: 63.9 us -> 63.2 us
    pallas_call x1, Pallas kernels: 62.6 us -> 61.9 us  [on_device(): pl.pallas_call(functools.partial(kernel, cfg), out_shape=jax.ShapeDtypeSt...]
where the time goes in v5:
time: 64.4 us; the launch traced here: 63.9 us
  Pallas kernels  63.2 us (98%)
    pallas_call x1, Pallas kernels, on_device(): pl.pallas_call(functools.partial(kernel, cfg), out_shape=jax.ShapeDtypeSt...  61.9 us
    pallas_call x1, Pallas kernels, on_device(): pl.pallas_call(functools.partial(tail, species, cy), out_shape=(jax.Shape...  1.37 us

profile of v5, /device:TPU:8, one launch (start us, length us, event | category | flops | bytes accessed | tf_op | source)
XLA Modules:
  0.0 63.9 jit_solution(3499201450512001696)
XLA Ops:
  0.6 61.9 %tucker_step.1.both = f32[64,128]{1,0:T(8,128)} custom-call(f32[33,168,128]{2,1,0:T(8,128)} %bitcast.5, f32[16,33]{1,0:T(8,128)} %bitcast.6), custom_call_target="tpu_custom_call" | custom-call | tf_op jit(solution)/shard_map/tucker_step/pallas_call | solution.py:372
  62.5 1.4 %parts.1 = (f32[16,33]{1,0:T(8,128)}, f32[42,42]{1,0:T(8,128)}) custom-call(f32[64,128]{1,0:T(8,128)} %tucker_step.1.both), custom_call_target="tpu_custom_call" | custom-call | tf_op jit(solution)/shard_map/parts/pallas_call | solution.py:383

commit v6 on v5

--- a/solution.py
+++ b/solution.py
@@ -22,6 +22,10 @@
 def split(value):
     high = value.astype(BF16)
     return high, (value - high.astype(F32)).astype(BF16)
+
+
+def far_first(n):
+    return sorted(range(1, n), key=lambda d: -min(d, n - d))
 
 
 def orth(w, ranks):
@@ -127,9 +131,9 @@
 
     pl.semaphore_wait(barrier, len(peers))
 
-    def start_sum(value, buf, n, me, target):
+    def start_sum(value, buf, offsets, me, target):
         buf[me] = value
-        return [send(buf.at[me], buf.at[me], target(d)) for d in range(1, n)]
+        return [send(buf.at[me], buf.at[me], target(d)) for d in offsets]
 
     def end_sum(copies, buf, n):
         for copy in copies:
@@ -139,9 +143,10 @@
             out = out + buf[k]
         return out
 
-    packed = end_sum(start_sum(packed, b_sa, ns, sa, to_sa), b_sa, ns)
-    packed = end_sum(start_sum(packed, b_p, nx * ny, gy, to_plane), b_p, nx * ny)
-    copies = start_sum(packed, b_z, nz, gx, to_z)
+    packed = end_sum(start_sum(packed, b_sa, [1], sa, to_sa), b_sa, ns)
+    plane = sorted(range(1, nx * ny), key=lambda d: -(min(d // nx, ny - d // nx) + min(d % nx, nx - d % nx)))
+    packed = end_sum(start_sum(packed, b_p, plane, gy, to_plane), b_p, nx * ny)
+    copies = start_sum(packed, b_z, far_first(nz), gx, to_z)
     w = wb[...]
     w = orth(orth(w, ranks), ranks)
     packed = end_sum(copies, b_z, nz)
@@ -185,13 +190,13 @@
     for a in range(hx):
         project(a)
         firsts[a] = []
-        for d in range(1, nx):
+        for d in far_first(nx):
             there = lax.rem(mx + d, nx)
             firsts[a].append(send(core.at[:, there, a, 0:cy], mid0.at[a, :, mx, 0:cy], to_x(d)))
         x = hx + a
         project(x)
         firsts[x] = []
-        for d in range(1, ny):
+        for d in far_first(ny):
             there = lax.rem(my + d, ny)
             firsts[x].append(send(core.at[there, :, x, 0:cy], mid1.at[a, :, my, 0:cy], to_y(d)))
     for a in range(hx):
@@ -203,7 +208,7 @@
         for copy in firsts[a]:
             copy.wait()
         seconds[a] = []
-        for d in range(1, ny):
+        for d in far_first(ny):
             there = lax.rem(my + d, ny)
             seconds[a].append(send(mid0.at[a, there, :, 0:cy], recv.at[a, my, :, 0:cy], to_y(d)))
         recv[a, my] = mid0[a, my]
@@ -211,7 +216,7 @@
         for copy in firsts[x]:
             copy.wait()
         seconds[x] = []
-        for d in range(1, nx):
+        for d in far_first(nx):
             there = lax.rem(mx + d, nx)
             seconds[x].append(send(mid1.at[a, there, :, 0:cy], recv.at[x, :, mx, 0:cy], to_x(d)))
         recv[x, :, mx] = mid1[a, mx]
@@ -250,7 +255,8 @@
     arrive(hx - 1)
 
     hy = YP // 2
-    order = [lax.rem(my + t, ny) for t in range(1, ny)] + [my]
+    offs = far_first(ny)
+    order = [lax.rem(my + d, ny) for d in offs] + [my]
     swaps, first0, first1 = [], {}, {}
 
     def theirs(t):
@@ -263,13 +269,13 @@
         mine = go[y] + gram_rows(y, sa, hx - 1)
         swaps[t].wait()
         go[y] = mine + gr[y]
-        for d in range(1, nx):
+        for d in far_first(nx):
             there = lax.rem(mx + d, nx)
             first0[t, d] = send(go.at[y, there, 0:hy, :], r1a.at[d - 1, y], to_x(d))
         if t < ny - 1:
-            for d in list(range(1, nx)) + [0]:
+            for d in far_first(nx) + [0]:
                 there = lax.rem(mx + d, nx)
-                first1[t, d] = send(go.at[y, there, hy:YP, :], r1b.at[t, there], to_y(t + 1))
+                first1[t, d] = send(go.at[y, there, hy:YP, :], r1b.at[t, there], to_y(offs[t]))
 
     theirs(0)
     for t in range(1, ny):
@@ -293,13 +299,12 @@
         return out
 
     second0, second1 = [], []
-    for k in range(max(nx, ny) - 1):
-        if k < ny - 1:
-            t0[k] = sum0(k)
-            second0.append(send(t0.at[k], r2a.at[k], to_y(k + 1)))
-        if k < nx - 1:
-            t1[k] = sum1(k + 1)
-            second1.append(send(t1.at[k], r2b.at[k], to_x(k + 1)))
+    for k in range(ny - 1):
+        t0[k] = sum0(k)
+        second0.append(send(t0.at[k], r2a.at[k], to_y(offs[k])))
+    for k, d in enumerate(far_first(nx)):
+        t1[k] = sum1(d)
+        second1.append(send(t1.at[k], r2b.at[k], to_x(d)))
     out0, out1 = sum0(ny - 1), sum1(0)
     for k in range(ny - 1):
         second0[k].wait()
@@ -326,7 +331,7 @@
         moved = jnp.where(lane < 2 * cy, pltpu.roll(parts[1], cy, 1), pltpu.roll(parts[2], 2 * cy, 1))
         pack[g] = jnp.where(lane < cy, parts[0], moved)
     last = []
-    for d in range(1, nz):
+    for d in far_first(nz):
         last.append(send(pack.at[lax.rem(gx + d, nz)], r3.at[d - 1], to_z(d)))
     out = pack[gx]
     for copy in last:

time: 64.4 us -> 62.9 us (0.977)
  Pallas kernels: 63.2 us -> 62.1 us
    pallas_call x1, Pallas kernels: 61.9 us -> 60.7 us  [on_device(): pl.pallas_call(functools.partial(kernel, cfg), out_shape=jax.ShapeDtypeSt...]
where the time goes in v6:
time: 62.9 us; the launch traced here: 62.7 us
  Pallas kernels  62.1 us (99%)
  between operations  0.64 us (1%)
    pallas_call x1, Pallas kernels, on_device(): pl.pallas_call(functools.partial(kernel, cfg), out_shape=jax.ShapeDtypeSt...  60.7 us
    pallas_call x1, Pallas kernels, on_device(): pl.pallas_call(functools.partial(tail, species, cy), out_shape=(jax.Shape...  1.37 us

profile of v6, /device:TPU:8, one launch (start us, length us, event | category | flops | bytes accessed | tf_op | source)
XLA Modules:
  0.0 62.7 jit_solution(3360425026003870263)
XLA Ops:
  0.6 60.7 %tucker_step.1.both = f32[64,128]{1,0:T(8,128)} custom-call(f32[33,168,128]{2,1,0:T(8,128)} %bitcast.5, f32[16,33]{1,0:T(8,128)} %bitcast.6), custom_call_target="tpu_custom_call" | custom-call | tf_op jit(solution)/shard_map/tucker_step/pallas_call | solution.py:377
  61.4 1.4 %parts.1 = (f32[16,33]{1,0:T(8,128)}, f32[42,42]{1,0:T(8,128)}) custom-call(f32[64,128]{1,0:T(8,128)} %tucker_step.1.both), custom_call_target="tpu_custom_call" | custom-call | tf_op jit(solution)/shard_map/parts/pallas_call | solution.py:388

commit v7 on v6

--- a/solution.py
+++ b/solution.py
@@ -11,7 +11,6 @@
 ITERS = 4
 F32 = jnp.float32
 BF16 = jnp.bfloat16
-HIGH = lax.Precision.HIGHEST
 LANES = 128
 SP = 48
 YP = 48
@@ -24,19 +23,22 @@
     return high, (value - high.astype(F32)).astype(BF16)
 
 
+def pieces(value):
+    lane = lax.broadcasted_iota(jnp.int32, value.shape, 1)
+    first = value.astype(BF16).astype(F32)
+    rest = value - first
+    second = rest.astype(BF16).astype(F32)
+    return jnp.where(lane < GROUP, first, jnp.where(lane < 2 * GROUP, second, rest - second)).astype(BF16)
+
+
 def far_first(n):
     return sorted(range(1, n), key=lambda d: -min(d, n - d))
 
 
 def orth(w, ranks):
     products = (w[:, None, :] * w[None, :, :]).reshape(ranks * ranks, LANES)
-    lane = lax.broadcasted_iota(jnp.int32, products.shape, 1)
-    first = products.astype(BF16).astype(F32)
-    rest = products - first
-    second = rest.astype(BF16).astype(F32)
-    pieces = jnp.where(lane < GROUP, first, jnp.where(lane < 2 * GROUP, second, rest - second))
     ones = jnp.ones((LANES, LANES), BF16)
-    inner = jnp.dot(pieces.astype(BF16), ones, preferred_element_type=F32)
+    inner = jnp.dot(pieces(products), ones, preferred_element_type=F32)
     lines = [inner[i * ranks : (i + 1) * ranks] for i in range(ranks)]
     row = lax.broadcasted_iota(jnp.int32, (ranks, LANES), 0)
     pivots = jnp.ones((ranks, LANES), F32)
@@ -163,8 +165,14 @@
     gram = upper + jnp.where(column >= (row & ~7) + 8, upper, 0.0).T
     gram = gram + pltpu.roll(gram, GROUP, 1) + pltpu.roll(gram, 2 * GROUP, 1)
 
+    gram = gram + pltpu.roll(gram, GROUP, 0) + pltpu.roll(gram, 2 * GROUP, 0)
+    first, rest = split(gram)
+    second, third = split(gram - first.astype(F32))
+    grams = jnp.concatenate([first, second, third], axis=1)
+
     def round_(i, w):
-        w = jnp.dot(w, gram, precision=HIGH, preferred_element_type=F32)
+        out = jnp.dot(pieces(w), grams, preferred_element_type=F32)
+        w = out[:, 0:LANES] + out[:, LANES : 2 * LANES] + out[:, 2 * LANES :]
         return orth(orth(w, ranks), ranks)
 
     w = lax.fori_loop(0, ITERS, round_, w)

time: 62.9 us -> 62.7 us (level)
  no operation moved by 1% of the time
where the time goes in v7:
time: 62.7 us; the launch traced here: 62.4 us
  Pallas kernels  61.8 us (99%)
  between operations  0.64 us (1%)
    pallas_call x1, Pallas kernels, on_device(): pl.pallas_call(functools.partial(kernel, cfg), out_shape=jax.ShapeDtypeSt...  60.4 us
    pallas_call x1, Pallas kernels, on_device(): pl.pallas_call(functools.partial(tail, species, cy), out_shape=(jax.Shape...  1.37 us

profile of v7, /device:TPU:8, one launch (start us, length us, event | category | flops | bytes accessed | tf_op | source)
XLA Modules:
  0.0 62.4 jit_solution(18053668507800665186)
XLA Ops:
  0.6 60.4 %tucker_step.1.both = f32[64,128]{1,0:T(8,128)} custom-call(f32[33,168,128]{2,1,0:T(8,128)} %bitcast.5, f32[16,33]{1,0:T(8,128)} %bitcast.6), custom_call_target="tpu_custom_call" | custom-call | tf_op jit(solution)/shard_map/tucker_step/pallas_call | solution.py:385
  61.1 1.4 %parts.1 = (f32[16,33]{1,0:T(8,128)}, f32[42,42]{1,0:T(8,128)}) custom-call(f32[64,128]{1,0:T(8,128)} %tucker_step.1.both), custom_call_target="tpu_custom_call" | custom-call | tf_op jit(solution)/shard_map/parts/pallas_call | solution.py:396
